TPU v7x, 128 devices: a whole 4x4x4 slice. The times are simulated.
128 devices in a mesh: req: 16 (over y, z), seq: 2 (over core), exp: 4 (over x).
Axes of the slice: x: 4, y: 4, z: 4, core: 2. Of those that a mesh axis runs over, the one named last changes fastest.
Arguments:
- residual: bfloat16 [256, 7168], P(('req', 'seq', 'exp')), may hold values from -6 to 6
- queries: bfloat16 [16, 16, 128, 576], P('req', None, 'exp'), may hold values from -60 to 60
- latent_cache: bfloat16 [16, 384, 576], P('req', 'seq'), may hold values from -20 to 20
- blocks: int32 [16, 2, 2], P('req', 'seq'), may hold values from 0 to 2, as said below
- lengths: int32 [16], P('req'), may hold values from 208 to 384, as said below
- value_up: bfloat16 [128, 512, 128], P('exp'), may hold values from -0.25 to 0.25
- out_proj: bfloat16 [16384, 7168], P('exp', ('req', 'seq')), may hold values from -0.046875 to 0.046875
- norm_gain: bfloat16 [7168], replicated, may hold values from 0.099609375 to 1.8984375
- router: bfloat16 [7168, 16], replicated, may hold values from -0.0625 to 0.0625
- expert_ids: int32 [256, 8], P(('req', 'seq', 'exp')), may hold values from 0 to 15, all different within a row; in each aligned block of 2 rows (0 to 1, 2 to 3, ...) at most 2 rows name the same one
- w_gate: bfloat16 [16, 7168, 2048], P('req', None, ('seq', 'exp')), may hold values from -0.0625 to 0.0625
- w_up: bfloat16 [16, 7168, 2048], P('req', None, ('seq', 'exp')), may hold values from -0.0625 to 0.0625
- w_down: bfloat16 [16, 2048, 7168], P('req', ('seq', 'exp')), may hold values from -0.125 to 0.125
Outputs:
- layer_out: bfloat16 [256, 7168], P(('req', 'seq', 'exp'))
Inputs may be any that keep to these rules, and one draw needn't show every extreme that they name: `blocks`: each request and shard lists 2 different block numbers of that shard. `lengths`: some request has exactly 384, some exactly 208. `expert_ids`: each row names 8 different experts; among the rows of one device (aligned blocks of 2 rows) no expert is named more than 2 times, a bound that some block reaches.
All inputs are finite; a program needn't handle non-finite values.
Results may differ from a plain program's by a relative error of at most 0.019.
Values may be sent and summed in bfloat16 or wider, within the bound.
No kernel may reach another device: no remote copies, remote signals or barrier semaphores. Data moves between devices by JAX's collectives and lax.ppermute only.
A program may use at most 128 MiB of HBM per device.

v0:
```python
import jax
import jax.numpy as jnp
from jax import lax
from jax.sharding import PartitionSpec as P

DL = 512
DR = 64
DV = 128
BLOCK = 64


def combined_all(x, axis, join):
    gathered = jax.tree.map(
        lambda a, kind: lax.all_gather(a.astype(kind), axis),
        x,
        (jnp.bfloat16, jnp.bfloat16, jnp.bfloat16),
    )

    def take(source):
        return jax.tree.map(
            lambda a, own: lax.dynamic_index_in_dim(a, source, 0, False).astype(own.dtype),
            gathered,
            x,
        )

    return lax.fori_loop(
        1, lax.axis_size(axis), lambda source, state: join(state, take(source)), take(0)
    )


def merge_parts(former, latter):
    row_max = jnp.maximum(former[0], latter[0])
    left_scale = jnp.exp(former[0] - row_max)
    right_scale = jnp.exp(latter[0] - row_max)
    return (
        row_max,
        left_scale * former[1] + right_scale * latter[1],
        left_scale[..., None] * former[2] + right_scale[..., None] * latter[2],
    )


def pick_rows(block_rows, picks):
    return block_rows[picks]


def shard_softmax(queries, picked, usable):
    scores = jnp.einsum("bqhk,bjk->bqhj", queries, picked, preferred_element_type=jnp.float32) * (
        DV + DR
    ) ** (-0.5)
    row_max = jnp.max(jnp.where(usable, scores, -1e30), axis=-1)
    weights = jnp.where(usable, jnp.exp(scores - row_max[..., None]), 0.0).astype(jnp.bfloat16)
    row_sum = jnp.sum(weights.astype(jnp.float32), -1)
    weighted = jnp.einsum(
        "bqhj,bjd->bqhd", weights, picked[..., :DL], preferred_element_type=jnp.float32
    )
    return (row_max, row_sum, weighted)


def expert_rows(arrived, w_gate, w_up, w_down):
    model_width = w_gate.shape[1]
    flat_rows = arrived.reshape(-1, model_width)
    gate_act = jnp.dot(flat_rows, w_gate[0], preferred_element_type=jnp.float32)
    up_act = jnp.dot(flat_rows, w_up[0], preferred_element_type=jnp.float32)
    activated = (jax.nn.silu(gate_act) * up_act).astype(jnp.bfloat16)
    partial_value = jnp.dot(activated, w_down[0], preferred_element_type=jnp.float32).astype(
        jnp.bfloat16
    )
    return partial_value.reshape(arrived.shape)


def per_device(
    residual,
    queries,
    latent_cache,
    blocks,
    lengths,
    value_up,
    out_proj,
    norm_gain,
    router,
    expert_ids,
    w_gate,
    w_up,
    w_down,
):
    local_reqs, drafts, head_count, qk_width = queries.shape
    shard_len = latent_cache.shape[1]
    picks_count = blocks.shape[2]
    seq_index = lax.axis_index("seq")
    block_view = latent_cache.reshape(local_reqs, shard_len // BLOCK, BLOCK, qk_width)
    picked = jax.vmap(pick_rows)(block_view, blocks[:, 0]).reshape(
        local_reqs, picks_count * BLOCK, qk_width
    )
    positions = (
        seq_index * shard_len + blocks[:, 0, :, None] * BLOCK + jnp.arange(BLOCK, dtype=jnp.int32)
    )
    positions = positions.reshape(local_reqs, picks_count * BLOCK)
    limits = lengths[:, None] - (drafts - 1) + jnp.arange(drafts, dtype=jnp.int32)[None, :]
    usable = positions[:, None, None, :] < limits[:, :, None, None]
    row_max, row_sum, weighted = shard_softmax(queries, picked, usable)
    row_max, row_sum, weighted = combined_all((row_max, row_sum, weighted), "seq", merge_parts)
    latent = (weighted / row_sum[..., None]).astype(jnp.bfloat16)
    head_values = jnp.einsum(
        "bqhd,hdv->bqhv", latent, value_up, preferred_element_type=jnp.float32
    ).astype(jnp.bfloat16)
    flat_values = head_values.reshape(local_reqs * drafts, head_count * DV)
    col_terms = jnp.dot(
        lax.all_gather(flat_values, "req", axis=0, tiled=True),
        out_proj,
        preferred_element_type=jnp.float32,
    )
    token_terms = lax.all_to_all(
        col_terms[None].astype(jnp.bfloat16),
        ("req", "seq", "exp"),
        split_axis=1,
        concat_axis=0,
        tiled=True,
    ).astype(jnp.float32)
    exp_count = lax.axis_size("exp")
    col_blocks = token_terms.shape[0] // exp_count
    rows_here = token_terms.shape[1]
    col_sums = jnp.sum(
        token_terms.reshape(col_blocks, exp_count, rows_here, token_terms.shape[2]), 1
    )
    attended = jnp.transpose(col_sums, (1, 0, 2)).reshape(rows_here, -1).astype(jnp.bfloat16)
    hidden_sum = (residual.astype(jnp.float32) + attended.astype(jnp.float32)).astype(jnp.bfloat16)
    hidden32 = hidden_sum.astype(jnp.float32)
    normed = (
        hidden32
        * lax.rsqrt(jnp.mean(hidden32 * hidden32, -1, keepdims=True) + 1e-06)
        * norm_gain.astype(jnp.float32)
    ).astype(jnp.bfloat16)
    gate_probs = jax.nn.sigmoid(jnp.dot(normed, router, preferred_element_type=jnp.float32))
    expert_count = router.shape[1]
    top_count = expert_ids.shape[1]
    one_hot = (expert_ids[:, :, None] == jnp.arange(expert_count, dtype=jnp.int32)).astype(
        jnp.int32
    )
    pair_hot = one_hot.reshape(rows_here * top_count, expert_count)
    slot_index = jnp.sum((jnp.cumsum(pair_hot, 0) - pair_hot) * pair_hot, -1)
    slot_hot = (slot_index[:, None] == jnp.arange(rows_here, dtype=jnp.int32)).astype(jnp.int32)
    placement = (pair_hot[:, :, None] * slot_hot[:, None, :]).reshape(
        rows_here, top_count, expert_count * rows_here
    )
    chosen = jnp.sum(one_hot.astype(jnp.float32) * gate_probs[:, None, :], -1)
    gate_weights = chosen / jnp.sum(chosen, -1, keepdims=True) * 2.5
    dispatch = jnp.sum(placement, 1).astype(jnp.bfloat16)
    outgoing = jnp.dot(dispatch.T, normed, preferred_element_type=jnp.float32).astype(jnp.bfloat16)
    outgoing = outgoing.reshape(expert_count, rows_here, outgoing.shape[1])
    combine = jnp.sum(gate_weights[:, :, None] * placement.astype(jnp.float32), 1)
    copies = lax.axis_size("seq") * exp_count
    fanned = jnp.broadcast_to(outgoing[:, None], (expert_count, copies) + outgoing.shape[1:])
    fanned = fanned.reshape((expert_count * copies,) + outgoing.shape[1:])
    returned = lax.all_to_all(
        expert_rows(
            lax.all_to_all(fanned, ("req", "seq", "exp"), split_axis=0, concat_axis=0, tiled=True),
            w_gate,
            w_up,
            w_down,
        ),
        ("req", "seq", "exp"),
        split_axis=0,
        concat_axis=0,
        tiled=True,
    )
    returned = returned.reshape((expert_count, copies) + outgoing.shape[1:]).astype(jnp.float32)
    expert_out = jnp.sum(returned, 1).astype(jnp.bfloat16)
    slot_rows = expert_out.reshape(expert_count * rows_here, expert_out.shape[2]).astype(
        jnp.float32
    )
    routed = jnp.dot(combine, slot_rows, precision=lax.Precision.HIGHEST)
    return (hidden32 + routed).astype(jnp.bfloat16)


def solution(mesh):
    in_specs = (
        P(("req", "seq", "exp"), None),
        P("req", None, "exp", None),
        P("req", "seq", None),
        P("req", "seq", None),
        P("req"),
        P("exp", None, None),
        P("exp", ("req", "seq")),
        P(),
        P(),
        P(("req", "seq", "exp"), None),
        P("req", None, ("seq", "exp")),
        P("req", None, ("seq", "exp")),
        P("req", ("seq", "exp"), None),
    )
    out_specs = P(("req", "seq", "exp"), None)
    return jax.shard_map(
        per_device, mesh=mesh, in_specs=in_specs, out_specs=out_specs, check_vma=False
    )
```

profile of v0, /device:TPU:1, one launch (start us, length us, event | category | flops | bytes accessed | tf_op | source)
XLA Modules:
  0.0 256.2 jit_solution(13494878136915248444)
XLA Ops:
  9.3 1.5 gather_fusion
  10.9 1.5 select_reduce_fusion
  12.4 1.2 convolution_convert_fusion.2
  13.9 2.9 %all-gather.2 = bf16[32,32]{1,0:T(8,128)(2,1)S(1)} all-gather(bf16[16,32]{1,0:T(8,128)(2,1)S(1)} %fusion.34), channel_id=4, replica_groups=mesh['req'=16,'seq'=2,'exp'=4] {'seq'}, dimensions={0}, use_global_device_ids=true | all-gather | bytes 3072 | tf_op jit(solution)/shard_map/all_gather | solution.py:14
  16.8 1.8 all-gather
  18.6 10.5 %all-gather.8.cloned.1.call-done = bf16[32,32,512]{2,1,0:T(8,128)(2,1)} async-done(((bf16[16,32,512]{2,1,0:T(8,128)(2,1)}), bf16[32,32,512]{2,1,0:T(8,128)(2,1)}) %all-gather.8.cloned.1.call-update) | async-done | bytes 1048592 | tf_op jit(solution)/shard_map/all_gather | solution.py:14
  29.1 1.5 fusion.22
  30.6 3.1 %fusion.15 = bf16[1,16,32,128]{3,1,2,0:T(8,128)(2,1)S(1)} fusion(bf16[32,512,128]{2,1,0:T(8,128)(2,1)} %param.18, bf16[16,32,512]{2,1,0:T(8,128)(2,1)S(1)} %fusion.22), kind=kOutput, calls=%fused_computation.18 | convolution fusion | flops 67174400 | bytes 4849664 | tf_op jit(solution)/shard_map/bqhd,hdv->bqhv/dot_general | solution.py:103
  35.0 44.1 %all-gather.6.cloned.1.call-done = bf16[256,4096]{1,0:T(8,128)(2,1)} async-done(((bf16[16,4096]{1,0:T(8,128)(2,1)}), bf16[256,4096]{1,0:T(8,128)(2,1)}) %all-gather.6.cloned.1.call-update) | async-done | bytes 2097168 | tf_op jit(solution)/shard_map/all_gather | solution.py:108
  79.1 2.4 fusion.16
  82.2 1.5 reduce.12
  84.3 9.1 %all-to-all-start = ((bf16[128,2,224]{2,1,0:T(2,128)(2,1)}), bf16[128,2,224]{2,1,0:T(2,128)(2,1)S(1)}, u32[]{:S(2)}, u32[]{:S(2)}) async-start(bf16[128,2,224]{2,1,0:T(2,128)(2,1)} %reshape.417), calls=%async_computation | async-start | bytes 262144 | tf_op jit(solution)/shard_map/all_to_all | solution.py:112
  94.2 9.3 %all-to-all-done = bf16[128,2,224]{2,1,0:T(2,128)(2,1)S(1)} async-done(((bf16[128,2,224]{2,1,0:T(2,128)(2,1)}), bf16[128,2,224]{2,1,0:T(2,128)(2,1)S(1)}, u32[]{:S(2)}, u32[]{:S(2)}) %all-to-all-start) | async-done | bytes 114720 | tf_op jit(solution)/shard_map/all_to_all | solution.py:112
  103.6 0.7 bitcast_reduce_fusion.1
  105.5 1.9 broadcast_in_dim.30
  107.4 51.8 %all_to_all.19 = bf16[128,2,7168]{2,1,0:T(2,128)(2,1)} all-to-all(bf16[128,2,7168]{2,1,0:T(2,128)(2,1)S(1)} %bitcast.72), channel_id=1, replica_groups=mesh['req'=16,'seq'=2,'exp'=4] {'req','seq','exp'}, dimensions={0} | all-to-all | bytes 7340032 | tf_op jit(solution)/shard_map/all_to_all | solution.py:156
  159.2 8.4 %reshape.371 = bf16[256,7168]{1,0:T(8,128)(2,1)} reshape(bf16[128,2,7168]{2,1,0:T(2,128)(2,1)} %all_to_all.19) | data formatting | bytes 7340032 | tf_op jit(solution)/shard_map/reshape | solution.py:61
  167.6 4.3 %fusion.4 = f32[256,256]{1,0:T(8,128)S(1)} fusion(bf16[256,7168]{1,0:T(8,128)(2,1)} %reshape.371, bf16[1,7168,256]{2,1,0:T(8,128)(2,1)} %param.23), kind=kOutput, calls=%fused_computation.9 | convolution fusion | flops 939524096 | bytes 7602176 | tf_op jit(solution)/shard_map/dot_general | solution.py:62
  171.9 10.0 %convolution_convert_fusion = bf16[256,7168]{1,0:T(8,128)(2,1)} fusion(bf16[1,256,7168]{2,1,0:T(8,128)(2,1)} %param.25, bf16[256,7168]{1,0:T(8,128)(2,1)} %reshape.371, bf16[1,7168,256]{2,1,0:T(8,128)(2,1)} %param.24, f32[256,256]{1,0:T(8,128)S(1)} %fusion.4), kind=kOutput, calls=%fused_computation.1 | convolution fusion | flops 1881276416 | bytes 14942208 | tf_op jit(solution)/shard_map/dot_general | solution.py:65
  181.9 8.1 %reshape.372 = bf16[128,2,7168]{2,1,0:T(2,128)(2,1)} reshape(bf16[256,7168]{1,0:T(8,128)(2,1)} %convolution_convert_fusion) | data formatting | bytes 7340032 | tf_op jit(solution)/shard_map/reshape | solution.py:68
  190.1 4.8 %all-to-all-start.2 = ((bf16[128,2,7168]{2,1,0:T(2,128)(2,1)}), bf16[128,2,7168]{2,1,0:T(2,128)(2,1)}, u32[]{:S(2)}, u32[]{:S(2)}) async-start(bf16[128,2,7168]{2,1,0:T(2,128)(2,1)} %reshape.372), calls=%async_computation.2 | async-start | bytes 7340032 | tf_op jit(solution)/shard_map/all_to_all | solution.py:154
  195.6 46.9 %all-to-all-done.2 = bf16[128,2,7168]{2,1,0:T(2,128)(2,1)} async-done(((bf16[128,2,7168]{2,1,0:T(2,128)(2,1)}), bf16[128,2,7168]{2,1,0:T(2,128)(2,1)}, u32[]{:S(2)}, u32[]{:S(2)}) %all-to-all-start.2) | async-done | bytes 3670048 | tf_op jit(solution)/shard_map/all_to_all | solution.py:154
  242.5 5.7 %bitcast_reduce_fusion = bf16[16,2,7168]{2,1,0:T(2,128)(2,1)S(1)} fusion(bf16[128,2,7168]{2,1,0:T(2,128)(2,1)} %all-to-all-done.2), kind=kLoop, calls=%fused_computation.5 | loop fusion | flops 1605632 | bytes 4128768 | tf_op jit(solution)/shard_map/reduce_sum | solution.py:167
  248.4 1.0 fusion
  (59 shorter events, 7.8 us)
Async XLA Ops:
  6.5 72.5 %copy-start = (bf16[4096,224]{0,1:T(8,128)(2,1)S(1)}, bf16[4096,224]{0,1:T(8,128)(2,1)}, u32[]{:S(2)}) copy-start(bf16[4096,224]{0,1:T(8,128)(2,1)} %param.19) | copy-start | bytes 5505028
  6.5 22.6 %all-gather.8.cloned.1.call-start = ((), (), s32[]{:S(2)}) async-start(), calls=%async_computation.4 | async-start | bytes 1572864 | tf_op jit(solution)/shard_map/all_gather | solution.py:14
  13.6 65.5 %all-gather.6.cloned.1.call-start = ((), (), s32[]{:S(2)}) async-start(), calls=%async_computation.3 | async-start | bytes 2228224 | tf_op jit(solution)/shard_map/all_gather | solution.py:108
  13.6 20.9 %copy-start.3 = (s32[2,8]{1,0:T(2,128)S(1)}, s32[2,8]{1,0:T(2,128)}, u32[]{:S(2)}) copy-start(s32[2,8]{1,0:T(2,128)} %param.22) | copy-start | bytes 196
  33.7 60.4 %copy-start.2 = (bf16[7168]{0:T(1024)(128)(2,1)S(1)}, bf16[7168]{0:T(1024)(128)(2,1)}, u32[]{:S(2)}) copy-start(bf16[7168]{0:T(1024)(128)(2,1)} %param.20) | copy-start | bytes 43012
  34.5 70.3 %copy-start.1 = (bf16[2,7168]{1,0:T(2,128)(2,1)S(1)}, bf16[2,7168]{1,0:T(2,128)(2,1)}, u32[]{:S(2)}) copy-start(bf16[2,7168]{1,0:T(2,128)(2,1)} %param.13) | copy-start | bytes 86020
  84.3 19.1 %all-to-all-start = ((bf16[128,2,224]{2,1,0:T(2,128)(2,1)}), bf16[128,2,224]{2,1,0:T(2,128)(2,1)S(1)}, u32[]{:S(2)}, u32[]{:S(2)}) async-start(bf16[128,2,224]{2,1,0:T(2,128)(2,1)} %reshape.417), calls=%async_computation | async-start | bytes 262144 | tf_op jit(solution)/shard_map/all_to_all | solution.py:112
  190.1 4.8 %copy-start.4 = (bf16[7168,16]{0,1:T(8,128)(2,1)S(1)}, bf16[7168,16]{0,1:T(8,128)(2,1)}, u32[]{:S(2)}) copy-start(bf16[7168,16]{0,1:T(8,128)(2,1)} %param.21) | copy-start | bytes 688132
  190.1 52.4 %all-to-all-start.2 = ((bf16[128,2,7168]{2,1,0:T(2,128)(2,1)}), bf16[128,2,7168]{2,1,0:T(2,128)(2,1)}, u32[]{:S(2)}, u32[]{:S(2)}) async-start(bf16[128,2,7168]{2,1,0:T(2,128)(2,1)} %reshape.372), calls=%async_computation.2 | async-start | bytes 7340032 | tf_op jit(solution)/shard_map/all_to_all | solution.py:154
Sparse Core Ops, SparseCore 0:
  13.7 15.3 all-gather.7
  34.6 44.4 all-gather.5
where the time goes:
time: 257 us; the launch traced here: 256 us
  waiting for transfers between devices  111 us (43%)
  blocking collectives  56.5 us (22%)
  local copies, waits for them, and re-layouts  24.2 us (9%)
  matrix products  24 us (9%)
  between operations  14.4 us (6%)
  starting transfers between devices  13.9 us (5%)
  other arithmetic  12.3 us (5%)
    all_to_all x1, blocking collectives, per_device(): lax.all_to_all(fanned, ('req', 'seq', 'exp'), split_axis=0, concat_axis=0...  51.8 us
    all_to_all x1, waiting for transfers between devices, per_device(): lax.all_to_all(expert_rows(lax.all_to_all(fanned, ('req', 'seq', 'exp'),...  46.9 us
    all_gather x1, waiting for transfers between devices, per_device(): lax.all_gather(flat_values, 'req', axis=0, tiled=True)  44.1 us
    all_gather x1, waiting for transfers between devices, combined_all(): lax.all_gather(a.astype(kind), axis)  10.5 us
    dot_general x1, matrix products, expert_rows(): jnp.dot(activated, w_down[0], preferred_element_type=jnp.float32)  10 us
    all_to_all x1, waiting for transfers between devices, per_device(): lax.all_to_all(col_terms[None].astype(jnp.bfloat16), ('req', 'seq', 'exp'...  9.29 us
    all_to_all x1, starting transfers between devices, per_device(): lax.all_to_all(col_terms[None].astype(jnp.bfloat16), ('req', 'seq', 'exp'...  9.06 us
    reshape x1, local copies, waits for them, and re-layouts, expert_rows(): flat_rows = arrived.reshape(-1, model_width)  8.4 us
  transfers between devices with their start and end apart: 4, of which 4 were waited for; matrix products, arithmetic and copies ran while one was open for 1% of the time, Pallas kernels for 0%

commit v1 on v0

--- a/solution.py
+++ b/solution.py
@@ -105,7 +105,9 @@
     ).astype(jnp.bfloat16)
     flat_values = head_values.reshape(local_reqs * drafts, head_count * DV)
     col_terms = jnp.dot(
-        lax.all_gather(flat_values, "req", axis=0, tiled=True),
+        jnp.concatenate(
+            lax.all_to_all(jnp.stack([flat_values] * lax.axis_size("req")), "req", 0, 0), axis=0
+        ),
         out_proj,
         preferred_element_type=jnp.float32,
     )

time: 257 us -> 249 us (0.969)
  waiting for transfers between devices: 111 us -> 95.6 us
  starting transfers between devices: 13.9 us -> 20.4 us
    all_gather x1 -> x0, waiting for transfers between devices: 44.1 us -> none  [per_device(): lax.all_gather(flat_values, 'req', axis=0, tiled=True)]
    all_to_all x0 -> x1, waiting for transfers between devices: none -> 28.8 us  [per_device(): lax.all_to_all(jnp.stack([flat_values] * lax.axis_size('req')), 'req', 0, 0)]
    all_to_all x0 -> x1, starting transfers between devices: none -> 6.85 us  [per_device(): lax.all_to_all(jnp.stack([flat_values] * lax.axis_size('req')), 'req', 0, 0)]
where the time goes in v1:
time: 249 us; the launch traced here: 248 us
  waiting for transfers between devices  95.6 us (38%)
  blocking collectives  56.5 us (23%)
  local copies, waits for them, and re-layouts  25.1 us (10%)
  matrix products  24 us (10%)
  starting transfers between devices  20.4 us (8%)
  between operations  14.5 us (6%)
  other arithmetic  12.3 us (5%)
    all_to_all x1, blocking collectives, per_device(): lax.all_to_all(fanned, ('req', 'seq', 'exp'), split_axis=0, concat_axis=0...  51.8 us
    all_to_all x1, waiting for transfers between devices, per_device(): lax.all_to_all(expert_rows(lax.all_to_all(fanned, ('req', 'seq', 'exp'),...  46.9 us
    all_to_all x1, waiting for transfers between devices, per_device(): lax.all_to_all(jnp.stack([flat_values] * lax.axis_size('req')), 'req', 0, 0)  28.8 us
    all_gather x1, waiting for transfers between devices, combined_all(): lax.all_gather(a.astype(kind), axis)  10.6 us
    dot_general x1, matrix products, expert_rows(): jnp.dot(activated, w_down[0], preferred_element_type=jnp.float32)  10 us
    all_to_all x1, waiting for transfers between devices, per_device(): lax.all_to_all(col_terms[None].astype(jnp.bfloat16), ('req', 'seq', 'exp'...  9.29 us
    all_to_all x1, starting transfers between devices, per_device(): lax.all_to_all(col_terms[None].astype(jnp.bfloat16), ('req', 'seq', 'exp'...  8.72 us
    reshape x1, local copies, waits for them, and re-layouts, expert_rows(): flat_rows = arrived.reshape(-1, model_width)  8.4 us
  transfers between devices with their start and end apart: 4, of which 4 were waited for; matrix products, arithmetic and copies ran while one was open for 1% of the time, Pallas kernels for 0%

profile of v1, /device:TPU:1, one launch (start us, length us, event | category | flops | bytes accessed | tf_op | source)
XLA Modules:
  0.0 248.3 jit_solution(14553822227825687819)
XLA Ops:
  9.3 1.5 gather_fusion
  10.9 1.5 select_reduce_fusion
  12.4 1.2 convolution_convert_fusion.2
  13.9 2.9 %all-gather.2 = bf16[32,32]{1,0:T(8,128)(2,1)S(1)} all-gather(bf16[16,32]{1,0:T(8,128)(2,1)S(1)} %fusion.34), channel_id=4, replica_groups=mesh['req'=16,'seq'=2,'exp'=4] {'seq'}, dimensions={0}, use_global_device_ids=true | all-gather | bytes 3072 | tf_op jit(solution)/shard_map/all_gather | solution.py:14
  16.7 1.8 all-gather
  18.5 10.6 %all-gather.5.cloned.1.call-done = bf16[32,32,512]{2,1,0:T(8,128)(2,1)} async-done(((bf16[16,32,512]{2,1,0:T(8,128)(2,1)}), bf16[32,32,512]{2,1,0:T(8,128)(2,1)}) %all-gather.5.cloned.1.call-update) | async-done | bytes 1048592 | tf_op jit(solution)/shard_map/all_gather | solution.py:14
  29.1 1.5 fusion.22
  30.6 3.1 %fusion.15 = bf16[1,16,32,128]{3,1,2,0:T(8,128)(2,1)S(1)} fusion(bf16[32,512,128]{2,1,0:T(8,128)(2,1)} %param.18, bf16[16,32,512]{2,1,0:T(8,128)(2,1)S(1)} %fusion.22), kind=kOutput, calls=%fused_computation.18 | convolution fusion | flops 67174400 | bytes 4849664 | tf_op jit(solution)/shard_map/bqhd,hdv->bqhv/dot_general | solution.py:103
  33.8 1.5 stack.3
  35.4 6.9 %all-to-all-start = ((bf16[16,16,4096]{2,1,0:T(8,128)(2,1)}), bf16[16,16,4096]{2,1,0:T(8,128)(2,1)}, u32[]{:S(2)}, u32[]{:S(2)}) async-start(bf16[16,16,4096]{2,1,0:T(8,128)(2,1)} %stack.3), calls=%async_computation | async-start | bytes 4194304 | tf_op jit(solution)/shard_map/all_to_all | solution.py:109
  42.7 28.8 %all-to-all-done = bf16[16,16,4096]{2,1,0:T(8,128)(2,1)} async-done(((bf16[16,16,4096]{2,1,0:T(8,128)(2,1)}), bf16[16,16,4096]{2,1,0:T(8,128)(2,1)}, u32[]{:S(2)}, u32[]{:S(2)}) %all-to-all-start) | async-done | bytes 2097184 | tf_op jit(solution)/shard_map/all_to_all | solution.py:109
  71.5 2.4 fusion.16
  74.6 1.5 reduce.12
  76.8 8.7 %all-to-all-start.1 = ((bf16[128,2,224]{2,1,0:T(2,128)(2,1)}), bf16[128,2,224]{2,1,0:T(2,128)(2,1)S(1)}, u32[]{:S(2)}, u32[]{:S(2)}) async-start(bf16[128,2,224]{2,1,0:T(2,128)(2,1)} %reshape.419), calls=%async_computation.1 | async-start | bytes 262144 | tf_op jit(solution)/shard_map/all_to_all | solution.py:114
  86.2 9.3 %all-to-all-done.1 = bf16[128,2,224]{2,1,0:T(2,128)(2,1)S(1)} async-done(((bf16[128,2,224]{2,1,0:T(2,128)(2,1)}), bf16[128,2,224]{2,1,0:T(2,128)(2,1)S(1)}, u32[]{:S(2)}, u32[]{:S(2)}) %all-to-all-start.1) | async-done | bytes 114720 | tf_op jit(solution)/shard_map/all_to_all | solution.py:114
  97.6 1.9 broadcast_in_dim.30
  99.5 51.8 %all_to_all.24 = bf16[128,2,7168]{2,1,0:T(2,128)(2,1)} all-to-all(bf16[128,2,7168]{2,1,0:T(2,128)(2,1)S(1)} %bitcast.73), channel_id=1, replica_groups=mesh['req'=16,'seq'=2,'exp'=4] {'req','seq','exp'}, dimensions={0} | all-to-all | bytes 7340032 | tf_op jit(solution)/shard_map/all_to_all | solution.py:158
  151.3 8.4 %reshape.373 = bf16[256,7168]{1,0:T(8,128)(2,1)} reshape(bf16[128,2,7168]{2,1,0:T(2,128)(2,1)} %all_to_all.24) | data formatting | bytes 7340032 | tf_op jit(solution)/shard_map/reshape | solution.py:61
  159.7 4.3 %fusion.4 = f32[256,256]{1,0:T(8,128)S(1)} fusion(bf16[256,7168]{1,0:T(8,128)(2,1)} %reshape.373, bf16[1,7168,256]{2,1,0:T(8,128)(2,1)} %param.23), kind=kOutput, calls=%fused_computation.9 | convolution fusion | flops 939524096 | bytes 7602176 | tf_op jit(solution)/shard_map/dot_general | solution.py:62
  164.0 10.0 %convolution_convert_fusion = bf16[256,7168]{1,0:T(8,128)(2,1)} fusion(bf16[1,256,7168]{2,1,0:T(8,128)(2,1)} %param.25, bf16[256,7168]{1,0:T(8,128)(2,1)} %reshape.373, bf16[1,7168,256]{2,1,0:T(8,128)(2,1)} %param.24, f32[256,256]{1,0:T(8,128)S(1)} %fusion.4), kind=kOutput, calls=%fused_computation.1 | convolution fusion | flops 1881276416 | bytes 14942208 | tf_op jit(solution)/shard_map/dot_general | solution.py:65
  174.0 8.1 %reshape.374 = bf16[128,2,7168]{2,1,0:T(2,128)(2,1)} reshape(bf16[256,7168]{1,0:T(8,128)(2,1)} %convolution_convert_fusion) | data formatting | bytes 7340032 | tf_op jit(solution)/shard_map/reshape | solution.py:68
  182.1 4.8 %all-to-all-start.3 = ((bf16[128,2,7168]{2,1,0:T(2,128)(2,1)}), bf16[128,2,7168]{2,1,0:T(2,128)(2,1)}, u32[]{:S(2)}, u32[]{:S(2)}) async-start(bf16[128,2,7168]{2,1,0:T(2,128)(2,1)} %reshape.374), calls=%async_computation.3 | async-start | bytes 7340032 | tf_op jit(solution)/shard_map/all_to_all | solution.py:156
  187.6 46.9 %all-to-all-done.3 = bf16[128,2,7168]{2,1,0:T(2,128)(2,1)} async-done(((bf16[128,2,7168]{2,1,0:T(2,128)(2,1)}), bf16[128,2,7168]{2,1,0:T(2,128)(2,1)}, u32[]{:S(2)}, u32[]{:S(2)}) %all-to-all-start.3) | async-done | bytes 3670048 | tf_op jit(solution)/shard_map/all_to_all | solution.py:156
  234.6 5.7 %bitcast_reduce_fusion = bf16[16,2,7168]{2,1,0:T(2,128)(2,1)S(1)} fusion(bf16[128,2,7168]{2,1,0:T(2,128)(2,1)} %all-to-all-done.3), kind=kLoop, calls=%fused_computation.5 | loop fusion | flops 1605632 | bytes 4128768 | tf_op jit(solution)/shard_map/reduce_sum | solution.py:169
  (59 shorter events, 8.8 us)
Async XLA Ops:
  6.5 65.0 %copy-start = (bf16[4096,224]{0,1:T(8,128)(2,1)S(1)}, bf16[4096,224]{0,1:T(8,128)(2,1)}, u32[]{:S(2)}) copy-start(bf16[4096,224]{0,1:T(8,128)(2,1)} %param.19) | copy-start | bytes 5505028
  6.5 22.6 %all-gather.5.cloned.1.call-start = ((), (), s32[]{:S(2)}) async-start(), calls=%async_computation.4 | async-start | bytes 1572864 | tf_op jit(solution)/shard_map/all_gather | solution.py:14
  33.7 8.5 %copy-start.3 = (s32[2,8]{1,0:T(2,128)S(1)}, s32[2,8]{1,0:T(2,128)}, u32[]{:S(2)}) copy-start(s32[2,8]{1,0:T(2,128)} %param.22) | copy-start | bytes 196
  35.4 36.1 %all-to-all-start = ((bf16[16,16,4096]{2,1,0:T(8,128)(2,1)}), bf16[16,16,4096]{2,1,0:T(8,128)(2,1)}, u32[]{:S(2)}, u32[]{:S(2)}) async-start(bf16[16,16,4096]{2,1,0:T(8,128)(2,1)} %stack.3), calls=%async_computation | async-start | bytes 4194304 | tf_op jit(solution)/shard_map/all_to_all | solution.py:109
  42.2 44.0 %copy-start.2 = (bf16[7168]{0:T(1024)(128)(2,1)S(1)}, bf16[7168]{0:T(1024)(128)(2,1)}, u32[]{:S(2)}) copy-start(bf16[7168]{0:T(1024)(128)(2,1)} %param.20) | copy-start | bytes 43012
  42.3 54.6 %copy-start.1 = (bf16[2,7168]{1,0:T(2,128)(2,1)S(1)}, bf16[2,7168]{1,0:T(2,128)(2,1)}, u32[]{:S(2)}) copy-start(bf16[2,7168]{1,0:T(2,128)(2,1)} %param.13) | copy-start | bytes 86020
  76.8 18.8 %all-to-all-start.1 = ((bf16[128,2,224]{2,1,0:T(2,128)(2,1)}), bf16[128,2,224]{2,1,0:T(2,128)(2,1)S(1)}, u32[]{:S(2)}, u32[]{:S(2)}) async-start(bf16[128,2,224]{2,1,0:T(2,128)(2,1)} %reshape.419), calls=%async_computation.1 | async-start | bytes 262144 | tf_op jit(solution)/shard_map/all_to_all | solution.py:114
  182.1 4.8 %copy-start.4 = (bf16[7168,16]{0,1:T(8,128)(2,1)S(1)}, bf16[7168,16]{0,1:T(8,128)(2,1)}, u32[]{:S(2)}) copy-start(bf16[7168,16]{0,1:T(8,128)(2,1)} %param.21) | copy-start | bytes 688132
  182.1 52.4 %all-to-all-start.3 = ((bf16[128,2,7168]{2,1,0:T(2,128)(2,1)}), bf16[128,2,7168]{2,1,0:T(2,128)(2,1)}, u32[]{:S(2)}, u32[]{:S(2)}) async-start(bf16[128,2,7168]{2,1,0:T(2,128)(2,1)} %reshape.374), calls=%async_computation.3 | async-start | bytes 7340032 | tf_op jit(solution)/shard_map/all_to_all | solution.py:156
Sparse Core Ops, SparseCore 0:
  13.7 15.3 all-gather.4
